TPU v7x, 32 devices: a whole 2x2x4 slice. The times are simulated.
32 devices in a mesh: layer: 8 (over z, x), land: 4 (over y, core).
Axes of the slice: x: 2, y: 2, z: 4, core: 2. Of those that a mesh axis runs over, the one named last changes fastest.
Arguments:
- gradients: bfloat16 [960, 65536], P(None, ('layer', 'land')), may hold values from -6 to 6
- queries: bfloat16 [32, 65536], P(None, ('layer', 'land')), may hold values from -6 to 6
- landmarks: bfloat16 [1024, 65536], P(None, ('layer', 'land')), may hold values from -0.0234375 to 0.0234375
- whitening: bfloat16 [1024, 1024], P(None, 'land'), may hold values from -2.5 to 2.5
Outputs:
- scores: float32 [32, 960], P('land', 'layer')
All inputs are finite; a program needn't handle non-finite values.
Results may differ from a plain program's by a relative error of at most 0.023.
Values may be sent and summed in bfloat16 or wider, within the bound.
A program may use at most 128 MiB of HBM per device.

v0:
```python
import jax
import jax.numpy as jnp
from jax import lax
from jax.sharding import PartitionSpec as P

LANDMARKS = 1024


def contract_rows(rows, piece):
    return lax.dot_general(
        rows, piece, (((1,), (1,)), ((), ())), preferred_element_type=jnp.float32
    )


def make_folder(example_rows, query_rows, piece):
    return (contract_rows(example_rows, piece), contract_rows(query_rows, piece))


def local(gradients, queries, landmarks, whitening):
    n_layer = lax.axis_size("layer")
    n_land = lax.axis_size("land")
    width = gradients.shape[1]
    rows_each = gradients.shape[0] // (n_layer * n_land)
    query_each = queries.shape[0] // (n_layer * n_land)
    split_ex = gradients.reshape(n_layer, n_land, rows_each, width)
    split_qr = queries.reshape(n_layer, n_land, query_each, width)
    moved_ex, moved_qr = (
        lax.all_to_all(split_ex, "land", split_axis=1, concat_axis=3, tiled=True),
        lax.all_to_all(split_qr, "land", split_axis=1, concat_axis=3, tiled=True),
    )
    layer_rows = moved_ex.reshape(n_layer * rows_each, n_land * width)
    layer_query = moved_qr.reshape(n_layer * query_each, n_land * width)
    partial_ex, partial_qr = make_folder(
        layer_rows, layer_query, lax.all_gather(landmarks, "land", axis=1, tiled=True)
    )
    share_ex, share_qr = (
        lax.psum_scatter(
            partial_ex.astype(jnp.bfloat16), "layer", scatter_dimension=0, tiled=True
        ).astype(jnp.float32),
        lax.psum_scatter(
            partial_qr.astype(jnp.bfloat16), "layer", scatter_dimension=0, tiled=True
        ).astype(jnp.float32),
    )
    projected, query_proj = (
        lax.all_gather(share_ex.astype(jnp.bfloat16), "land", axis=0, tiled=True),
        lax.all_gather(share_qr.astype(jnp.bfloat16), "land", axis=0, tiled=True),
    )
    whitened = jnp.dot(projected, whitening, preferred_element_type=jnp.float32).astype(
        jnp.bfloat16
    )
    query_white = jnp.dot(query_proj, whitening, preferred_element_type=jnp.float32).astype(
        jnp.bfloat16
    )
    all_queries = lax.all_gather(query_white, "layer", axis=0, tiled=True)
    factor = LANDMARKS ** (-0.5)
    return lax.psum_scatter(
        (contract_rows(all_queries, whitened) * factor).astype(jnp.bfloat16),
        "land",
        scatter_dimension=0,
        tiled=True,
    ).astype(jnp.float32)


def solution(mesh):
    return jax.shard_map(
        local,
        mesh=mesh,
        in_specs=(
            P(None, ("layer", "land")),
            P(None, ("layer", "land")),
            P(None, ("layer", "land")),
            P(None, "land"),
        ),
        out_specs=P("land", "layer"),
        check_vma=False,
    )
```

profile of v0, /device:TPU:0, one launch (start us, length us, event | category | flops | bytes accessed | tf_op | source)
XLA Modules:
  0.0 296.0 jit_solution(8832669708729953579)
XLA Ops:
  6.5 0.0 copy-start
  6.5 0.0 all-gather.5.cloned.1.call-start
  6.5 0.7 all-gather.5.cloned.1.call-update
  7.3 5.0 %reshape.19 = bf16[8,4,30,2048]{3,2,1,0:T(8,128)(2,1)} reshape(bf16[960,2048]{1,0:T(8,128)(2,1)} %param.4) | data formatting | bytes 7864320 | tf_op jit(solution)/shard_map/reshape | solution.py:25
  12.3 6.4 %copy.9 = bf16[8,4,30,2048]{3,0,2,1:T(8,128)(2,1)} copy(bf16[8,4,30,2048]{3,2,1,0:T(8,128)(2,1)} %reshape.19) | data formatting | bytes 7864320 | tf_op jit(solution)/shard_map/reshape | solution.py:25
  18.7 0.0 copy-start.1
  18.7 0.0 copy-start.3
  18.7 0.0 copy-start.2
  18.7 5.1 %all-to-all-start.1 = ((bf16[8,4,30,2048]{3,0,2,1:T(8,128)(2,1)}), bf16[8,4,30,2048]{3,0,2,1:T(8,128)(2,1)}, u32[]{:S(2)}, u32[]{:S(2)}) async-start(bf16[8,4,30,2048]{3,0,2,1:T(8,128)(2,1)} %copy.9), calls=%async_computation.1 | async-start | bytes 7864320 | tf_op jit(solution)/shard_map/all_to_all | solution.py:28
  23.8 0.0 copy-done.1
  23.8 0.1 reshape.17
  23.9 0.7 copy.8
  24.6 0.0 copy-done.3
  24.6 0.6 dynamic-slice.4
  25.2 0.0 copy-done.2
  25.2 0.7 fusion.7
  27.1 85.5 %all-to-all-done.1 = bf16[8,4,30,2048]{3,0,2,1:T(8,128)(2,1)} async-done(((bf16[8,4,30,2048]{3,0,2,1:T(8,128)(2,1)}), bf16[8,4,30,2048]{3,0,2,1:T(8,128)(2,1)}, u32[]{:S(2)}, u32[]{:S(2)}) %all-to-all-start.1) | async-done | bytes 3932192 | tf_op jit(solution)/shard_map/all_to_all | solution.py:28
  112.6 3.5 %all-to-all-start = ((bf16[8,4,1,2048]{3,0,2,1:T(8,128)(2,1)}), bf16[8,4,1,2048]{3,0,2,1:T(8,128)(2,1)S(1)}, u32[]{:S(2)}, u32[]{:S(2)}) async-start(bf16[8,4,1,2048]{3,0,2,1:T(8,128)(2,1)} %copy.8), calls=%async_computation | async-start | bytes 262144 | tf_op jit(solution)/shard_map/all_to_all | solution.py:29
  116.1 5.1 %copy.10 = bf16[8,1,30,4,2048]{4,3,2,0,1:T(4,128)(2,1)S(1)} copy(bf16[8,1,30,4,2048]{4,0,2,3,1:T(8,128)(2,1)} %bitcast.4) | data formatting | bytes 7864320 | tf_op jit(solution)/shard_map/all_to_all | solution.py:28
  121.2 6.0 %copy.12 = bf16[30,8,4,2048]{3,1,2,0:T(8,128)(2,1)} copy(bf16[30,8,4,2048]{3,2,1,0:T(4,128)(2,1)S(1)} %bitcast.29) | data formatting | bytes 7864320
  127.2 33.9 %all-gather.5.cloned.1.call-done = bf16[1024,8192]{1,0:T(8,128)(2,1)} async-done(((bf16[1024,2048]{1,0:T(8,128)(2,1)}), bf16[1024,8192]{1,0:T(8,128)(2,1)}) %all-gather.5.cloned.1.call-update) | async-done | bytes 16777232 | tf_op jit(solution)/shard_map/all_gather | solution.py:34
  161.1 11.5 %convolution_convert_fusion = bf16[240,1024]{1,0:T(8,128)(2,1)S(1)} fusion(bf16[240,8192]{1,0:T(8,128)(2,1)} %bitcast.30, bf16[1024,8192]{1,0:T(8,128)(2,1)} %all-gather.5.cloned.1.call-done), kind=kOutput, calls=%fused_computation | convolution fusion | flops 4026777600 | bytes 21200896 | tf_op jit(solution)/shard_map/dot_general | solution.py:10
  172.6 25.3 %fusion = bf16[32,1024]{1,0:T(8,128)(2,1)S(1)} fusion(bf16[240,1024]{1,0:T(8,128)(2,1)S(1)} %convolution_convert_fusion), kind=kCustom, calls=%all-reduce-scatter | all-reduce-scatter fusion | flops 262145 | bytes 557568
  197.9 2.1 collective-permute-start
  200.0 0.0 all-to-all-done
  200.0 10.2 %convolution_convert_fusion.2 = bf16[8,1024]{1,0:T(8,128)(2,1)S(1)} fusion(bf16[8,8192]{1,0:T(8,128)(2,1)S(1)} %bitcast.31, bf16[1024,8192]{1,0:T(8,128)(2,1)} %all-gather.5.cloned.1.call-done), kind=kOutput, calls=%fused_computation.3 | convolution fusion | flops 134225920 | bytes 16924672 | tf_op jit(solution)/shard_map/dot_general | solution.py:10
  210.2 33.6 %all-reduce = bf16[8,1024]{1,0:T(8,128)(2,1)S(1)} all-reduce(bf16[8,1024]{1,0:T(8,128)(2,1)S(1)} %convolution_convert_fusion.2), channel_id=2, replica_groups=mesh['layer'=8,'land'=4] {'layer'}, use_global_device_ids=true, to_apply=%region_0.0.clone | all-reduce | flops 8192 | bytes 32768
  243.8 0.6 dynamic-slice_bitcast_fusion.1
  244.4 5.2 %all-gather = bf16[4,1,1024]{2,1,0:T(2,128)(2,1)S(1)} all-gather(bf16[1,1,1024]{2,1,0:T(2,128)(2,1)S(1)} %dynamic-slice_bitcast_fusion.1), channel_id=1, replica_groups=mesh['layer'=8,'land'=4] {'land'}, dimensions={0}, use_global_device_ids=true | all-gather | bytes 10240 | tf_op jit(solution)/shard_map/all_gather | solution.py:46
  249.6 0.0 copy-done
  249.6 0.2 fusion.4
  249.8 26.0 %all-gather.1 = bf16[8,4,256]{2,1,0:T(4,128)(2,1)S(1)} all-gather(bf16[1,4,256]{2,1,0:T(4,128)(2,1)S(1)} %fusion.4), channel_id=1, replica_groups=mesh['layer'=8,'land'=4] {'layer'}, dimensions={0}, use_global_device_ids=true | all-gather | bytes 18432 | tf_op jit(solution)/shard_map/all_gather | solution.py:54
  275.8 0.0 collective-permute-done
  275.8 0.2 concatenate
  276.1 5.8 %all-gather.2 = bf16[4,30,1024]{2,1,0:T(8,128)(2,1)S(1)} all-gather(bf16[1,30,1024]{2,1,0:T(8,128)(2,1)S(1)} %dynamic-slice_bitcast_fusion), channel_id=1, replica_groups=mesh['layer'=8,'land'=4] {'land'}, dimensions={0}, use_global_device_ids=true | all-gather | bytes 307200 | tf_op jit(solution)/shard_map/all_gather | solution.py:45
  281.9 0.1 reshape.26
  281.9 0.3 fusion.3
  282.3 6.2 %all-reduce.2 = bf16[32,120]{1,0:T(8,128)(2,1)S(1)} all-reduce(bf16[32,120]{1,0:T(8,128)(2,1)S(1)} %fusion.3), channel_id=4, replica_groups=mesh['layer'=8,'land'=4] {'land'}, use_global_device_ids=true, to_apply=%region_2.0.clone | all-reduce | flops 3840 | bytes 15360
  288.5 0.6 dynamic-slice_convert_fusion
  (3 shorter events, 0.1 us)
Async XLA Ops:
  6.5 243.1 %copy-start = (bf16[1024,256]{1,0:T(8,128)(2,1)S(1)}, bf16[1024,256]{1,0:T(8,128)(2,1)}, u32[]{:S(2)}) copy-start(bf16[1024,256]{1,0:T(8,128)(2,1)} %param.7) | copy-start | bytes 1572868
  6.5 154.6 %all-gather.5.cloned.1.call-start = ((), (), s32[]{:S(2)}) async-start(), calls=%async_computation.2 | async-start | bytes 20971520 | tf_op jit(solution)/shard_map/all_gather | solution.py:34
  18.7 5.1 %copy-start.1 = (bf16[32,2048]{1,0:T(8,128)(2,1)S(1)}, bf16[32,2048]{1,0:T(8,128)(2,1)}, u32[]{:S(2)}) copy-start(bf16[32,2048]{1,0:T(8,128)(2,1)} %param.5) | copy-start | bytes 393220
  18.7 6.0 %copy-start.3 = (u32[32]{0:T(128)S(1)}, u32[32]{0:T(128)}, u32[]{:S(2)}) copy-start(u32[32]{0:T(128)} %constant.12) | copy-start | bytes 388
  18.7 6.5 %copy-start.2 = (u32[32]{0:T(128)S(1)}, u32[32]{0:T(128)}, u32[]{:S(2)}) copy-start(u32[32]{0:T(128)} %constant.4) | copy-start | bytes 388
  18.7 93.9 %all-to-all-start.1 = ((bf16[8,4,30,2048]{3,0,2,1:T(8,128)(2,1)}), bf16[8,4,30,2048]{3,0,2,1:T(8,128)(2,1)}, u32[]{:S(2)}, u32[]{:S(2)}) async-start(bf16[8,4,30,2048]{3,0,2,1:T(8,128)(2,1)} %copy.9), calls=%async_computation.1 | async-start | bytes 7864320 | tf_op jit(solution)/shard_map/all_to_all | solution.py:28
  112.6 87.4 %all-to-all-start = ((bf16[8,4,1,2048]{3,0,2,1:T(8,128)(2,1)}), bf16[8,4,1,2048]{3,0,2,1:T(8,128)(2,1)S(1)}, u32[]{:S(2)}, u32[]{:S(2)}) async-start(bf16[8,4,1,2048]{3,0,2,1:T(8,128)(2,1)} %copy.8), calls=%async_computation | async-start | bytes 262144 | tf_op jit(solution)/shard_map/all_to_all | solution.py:29
  197.9 77.9 %collective-permute-start = (bf16[14,1024]{1,0:T(8,128)(2,1)S(1)}, bf16[14,1024]{1,0:T(8,128)(2,1)S(1)}, u32[]{:S(2)}, u32[]{:S(2)}) collective-permute-start(bf16[14,1024]{1,0:T(8,128)(2,1)S(1)} %slice), channel_id=1, source_target_pairs={{0,4},{4,8},{8,12},{12,16},{16,20},{20,24},{24,28},{1,5},{5,9},{9,... | collective-permute-start | bytes 86024
Sparse Core Ops, SparseCore 0:
  8.9 152.1 all-gather.4
where the time goes:
time: 297 us; the launch traced here: 296 us
  waiting for transfers between devices  120 us (40%)
  blocking collectives  102 us (34%)
  local copies, waits for them, and re-layouts  25.6 us (9%)
  matrix products  22.2 us (7%)
  between operations  14.8 us (5%)
  starting transfers between devices  10.7 us (4%)
    all_to_all x1, waiting for transfers between devices, local(): lax.all_to_all(split_ex, 'land', split_axis=1, concat_axis=3, tiled=True)  85.5 us
    unnamed x3, blocking collectives  65.1 us
    all_gather x1, waiting for transfers between devices, local(): lax.all_gather(landmarks, 'land', axis=1, tiled=True)  33.9 us
    all_gather x1, blocking collectives, local(): all_queries = lax.all_gather(query_white, 'layer', axis=0, tiled=True)  26 us
    dot_general x3, matrix products, contract_rows(): lax.dot_general(rows, piece, (((1,), (1,)), ((), ())), preferred_element_...  22 us
    reshape x2, local copies, waits for them, and re-layouts, local(): split_ex = gradients.reshape(n_layer, n_land, rows_each, width)  11.4 us
    unnamed x17, local copies, waits for them, and re-layouts  8.18 us
  transfers between devices with their start and end apart: 4, of which 2 were waited for; matrix products, arithmetic and copies ran while one was open for 24% of the time, Pallas kernels for 0%

commit v1 on v0

--- a/solution.py
+++ b/solution.py
@@ -4,6 +4,27 @@
 from jax.sharding import PartitionSpec as P
 
 LANDMARKS = 1024
+
+
+def gather_around(shard, axis, dim):
+    devices, index, rows = (lax.axis_size(axis), lax.axis_index(axis), shard.shape[dim])
+    right = [(i, (i + 1) % devices) for i in range(devices)]
+    backward = [(i, (i - 1) % devices) for i in range(devices)]
+    filled = jnp.zeros((*shard.shape[:dim], devices * rows, *shard.shape[dim + 1 :]), shard.dtype)
+    filled = lax.dynamic_update_slice_in_dim(filled, shard, index * rows, axis=dim)
+    from_left = from_right = shard
+    half = devices // 2
+    for hop in range(1, half + 1):
+        from_left = lax.ppermute(from_left, axis, right)
+        filled = lax.dynamic_update_slice_in_dim(
+            filled, from_left, (index - hop) % devices * rows, axis=dim
+        )
+        if hop < devices - half:
+            from_right = lax.ppermute(from_right, axis, backward)
+            filled = lax.dynamic_update_slice_in_dim(
+                filled, from_right, (index + hop) % devices * rows, axis=dim
+            )
+    return filled
 
 
 def contract_rows(rows, piece):
@@ -31,7 +52,7 @@
     layer_rows = moved_ex.reshape(n_layer * rows_each, n_land * width)
     layer_query = moved_qr.reshape(n_layer * query_each, n_land * width)
     partial_ex, partial_qr = make_folder(
-        layer_rows, layer_query, lax.all_gather(landmarks, "land", axis=1, tiled=True)
+        layer_rows, layer_query, gather_around(landmarks, "land", 1)
     )
     share_ex, share_qr = (
         lax.psum_scatter(

time: 297 us -> 337 us (1.13)
  local copies, waits for them, and re-layouts: 25.6 us -> 46.5 us
  waiting for transfers between devices: 120 us -> 138 us
  starting transfers between devices: 10.7 us -> 27.7 us
  between operations: 14.8 us -> 1.41 us
    ppermute x0 -> x3, waiting for transfers between devices: none -> 88.7 us  [the longest x2 88.7 us: gather_around(): from_left = lax.ppermute(from_left, axis, right)]
    all_to_all x1, waiting for transfers between devices: 85.5 us -> 49 us  [local(): lax.all_to_all(split_ex, 'land', split_axis=1, concat_axis=3, tiled=True)]
    all_gather x1 -> x0, waiting for transfers between devices: 33.9 us -> none  [local(): lax.all_gather(landmarks, 'land', axis=1, tiled=True)]
    dynamic_update_slice x0 -> x4, local copies, waits for them, and re-layouts: none -> 16.3 us  [the longest x2 9.39 us: gather_around(): lax.dynamic_update_slice_in_dim(filled, from_left, (index - hop) % device...]
    all_to_all x1, starting transfers between devices: 3.5 us -> 16.1 us  [local(): lax.all_to_all(split_qr, 'land', split_axis=1, concat_axis=3, tiled=True)]
    broadcast_in_dim x0 -> x1, local copies, waits for them, and re-layouts: none -> 6.65 us  [gather_around(): jnp.zeros((*shard.shape[:dim], devices * rows, *shard.shape[dim + 1:]), s...]
    ppermute x0 -> x3, starting transfers between devices: none -> 5.04 us  [the longest x2 3.02 us: gather_around(): from_left = lax.ppermute(from_left, axis, right)]
    unnamed x17 -> x19, local copies, waits for them, and re-layouts: 8.18 us -> 6.34 us
  transfers between devices with their start and end apart: 4 -> 6, of which waited for: 2 -> 2; matrix products, arithmetic and copies ran while one was open for 24% -> 27% of each run, Pallas kernels for 0% -> 0%
where the time goes in v1:
time: 337 us; the launch traced here: 336 us
  waiting for transfers between devices  138 us (41%)
  blocking collectives  103 us (31%)
  local copies, waits for them, and re-layouts  46.5 us (14%)
  starting transfers between devices  27.7 us (8%)
  matrix products  18.9 us (6%)
    ppermute x2, waiting for transfers between devices, gather_around(): from_left = lax.ppermute(from_left, axis, right)  88.7 us
    unnamed x3, blocking collectives  65.9 us
    all_to_all x1, waiting for transfers between devices, local(): lax.all_to_all(split_ex, 'land', split_axis=1, concat_axis=3, tiled=True)  49 us
    all_gather x1, blocking collectives, local(): all_queries = lax.all_gather(query_white, 'layer', axis=0, tiled=True)  26 us
    dot_general x3, matrix products, contract_rows(): lax.dot_general(rows, piece, (((1,), (1,)), ((), ())), preferred_element_...  18.7 us
    all_to_all x1, starting transfers between devices, local(): lax.all_to_all(split_qr, 'land', split_axis=1, concat_axis=3, tiled=True)  16.1 us
    reshape x2, local copies, waits for them, and re-layouts, local(): split_ex = gradients.reshape(n_layer, n_land, rows_each, width)  11.3 us
    dynamic_update_slice x2, local copies, waits for them, and re-layouts, gather_around(): lax.dynamic_update_slice_in_dim(filled, from_left, (index - hop) % device...  9.39 us
  transfers between devices with their start and end apart: 6, of which 2 were waited for; matrix products, arithmetic and copies ran while one was open for 27% of the time, Pallas kernels for 0%

profile of v1, /device:TPU:0, one launch (start us, length us, event | category | flops | bytes accessed | tf_op | source)
XLA Modules:
  0.0 336.2 jit_solution(8066812109803627216)
XLA Ops:
  0.0 0.0 copy-start
  0.0 0.0 copy-start.4
  0.0 0.0 copy-start.3
  0.0 0.0 copy-start.2
  0.0 0.5 collective-permute-start
  0.5 2.0 collective-permute-start.1
  2.6 88.7 %collective-permute-done = bf16[1024,2048]{1,0:T(8,128)(2,1)} collective-permute-done((bf16[1024,2048]{1,0:T(8,128)(2,1)}, bf16[1024,2048]{1,0:T(8,128)(2,1)}, u32[]{:S(2)}, u32[]{:S(2)}) %collective-permute-start) | collective-permute-done | bytes 4194336 | tf_op jit(solution)/shard_map/ppermute | solution.py:18
  91.3 2.5 collective-permute-start.2
  93.8 5.0 %reshape.19 = bf16[8,4,30,2048]{3,2,1,0:T(8,128)(2,1)} reshape(bf16[960,2048]{1,0:T(8,128)(2,1)} %param.4) | data formatting | bytes 7864320 | tf_op jit(solution)/shard_map/reshape | solution.py:46
  98.8 6.2 %copy.9 = bf16[8,4,30,2048]{3,0,2,1:T(8,128)(2,1)} copy(bf16[8,4,30,2048]{3,2,1,0:T(8,128)(2,1)} %reshape.19) | data formatting | bytes 7864320 | tf_op jit(solution)/shard_map/reshape | solution.py:46
  105.0 4.8 %all-to-all-start.1 = ((bf16[8,4,30,2048]{3,0,2,1:T(8,128)(2,1)}), bf16[8,4,30,2048]{3,0,2,1:T(8,128)(2,1)}, u32[]{:S(2)}, u32[]{:S(2)}) async-start(bf16[8,4,30,2048]{3,0,2,1:T(8,128)(2,1)} %copy.9), calls=%async_computation.1 | async-start | bytes 7864320 | tf_op jit(solution)/shard_map/all_to_all | solution.py:49
  109.9 0.0 copy-done.2
  110.0 0.1 reshape.17
  110.0 0.7 copy.8
  110.8 0.0 copy-done.4
  110.8 0.6 dynamic-slice.4
  111.3 0.0 copy-done.3
  111.3 0.7 fusion.9
  113.2 0.0 copy-start.1
  113.2 6.6 %broadcast_in_dim.3 = bf16[1024,8192]{1,0:T(8,128)(2,1)} broadcast(bf16[]{:T(256)} %constant.30.clone.1), dimensions={} | broadcast | bytes 16777218 | tf_op jit(solution)/shard_map/broadcast_in_dim | solution.py:13
  119.9 0.0 copy-done.1
  119.9 2.2 constant_dynamic-update-slice_fusion.3
  122.1 49.0 %all-to-all-done.1 = bf16[8,4,30,2048]{3,0,2,1:T(8,128)(2,1)} async-done(((bf16[8,4,30,2048]{3,0,2,1:T(8,128)(2,1)}), bf16[8,4,30,2048]{3,0,2,1:T(8,128)(2,1)}, u32[]{:S(2)}, u32[]{:S(2)}) %all-to-all-start.1) | async-done | bytes 3932192 | tf_op jit(solution)/shard_map/all_to_all | solution.py:49
  171.1 16.1 %all-to-all-start = ((bf16[8,4,1,2048]{3,0,2,1:T(8,128)(2,1)}), bf16[8,4,1,2048]{3,0,2,1:T(8,128)(2,1)S(1)}, u32[]{:S(2)}, u32[]{:S(2)}) async-start(bf16[8,4,1,2048]{3,0,2,1:T(8,128)(2,1)} %copy.8), calls=%async_computation | async-start | bytes 262144 | tf_op jit(solution)/shard_map/all_to_all | solution.py:50
  187.2 5.1 %copy.10 = bf16[8,1,30,4,2048]{4,3,2,0,1:T(4,128)(2,1)S(1)} copy(bf16[8,1,30,4,2048]{4,0,2,3,1:T(8,128)(2,1)} %bitcast.5) | data formatting | bytes 7864320 | tf_op jit(solution)/shard_map/all_to_all | solution.py:49
  192.4 4.1 %copy.12 = bf16[30,8,4,2048]{3,1,2,0:T(8,128)(2,1)S(1)} copy(bf16[30,8,4,2048]{3,2,1,0:T(4,128)(2,1)S(1)} %bitcast.33) | data formatting | bytes 7864320
  196.5 4.7 %constant_dynamic-update-slice_fusion.2 = bf16[1024,8192]{1,0:T(8,128)(2,1)} fusion(bf16[1024,8192]{1,0:T(8,128)(2,1)} %constant_dynamic-update-slice_fusion.3, bf16[1024,2048]{1,0:T(8,128)(2,1)} %collective-permute-done, s32[]{:T(128)S(6)} %select_n.29), kind=kLoop, calls=%fused_computation.17 | loop fusion | bytes 8388612 | tf_op jit(solution)/shard_map/dynamic_update_slice | solution.py:19
  201.2 0.0 collective-permute-done.1
  201.2 4.7 %constant_dynamic-update-slice_fusion.1 = bf16[1024,8192]{1,0:T(8,128)(2,1)} fusion(bf16[1024,8192]{1,0:T(8,128)(2,1)} %constant_dynamic-update-slice_fusion.2, bf16[1024,2048]{1,0:T(8,128)(2,1)} %collective-permute-done.1, s32[]{:T(128)S(6)} %select_n.31), kind=kLoop, calls=%fused_computation.16 | loop fusion | bytes 8388612 | tf_op jit(solution)/shard_map/dynamic_update_slice | solution.py:24
  205.9 0.0 collective-permute-done.2
  205.9 4.7 %constant_dynamic-update-slice_fusion = bf16[1024,8192]{1,0:T(8,128)(2,1)} fusion(bf16[1024,8192]{1,0:T(8,128)(2,1)} %constant_dynamic-update-slice_fusion.1, bf16[1024,2048]{1,0:T(8,128)(2,1)} %collective-permute-done.2, s32[]{:T(128)S(6)} %select_n.33), kind=kLoop, calls=%fused_computation.15 | loop fusion | bytes 8388612 | tf_op jit(solution)/shard_map/dynamic_update_slice | solution.py:19
  210.6 8.2 %fusion.1 = bf16[240,1024]{1,0:T(8,128)(2,1)S(1)} fusion(bf16[1024,8192]{1,0:T(8,128)(2,1)} %constant_dynamic-update-slice_fusion, bf16[240,8192]{1,0:T(8,128)(2,1)S(1)} %bitcast.34), kind=kOutput, calls=%fused_computation.1 | convolution fusion | flops 4026777600 | bytes 21200896 | tf_op jit(solution)/shard_map/dot_general | solution.py:31
  218.8 25.1 %fusion = bf16[32,1024]{1,0:T(8,128)(2,1)S(1)} fusion(bf16[240,1024]{1,0:T(8,128)(2,1)S(1)} %fusion.1), kind=kCustom, calls=%all-reduce-scatter | all-reduce-scatter fusion | flops 262145 | bytes 557568
  243.9 1.8 collective-permute-start.3
  245.6 0.0 all-to-all-done
  245.7 10.2 %fusion.3 = bf16[8,1024]{1,0:T(8,128)(2,1)S(1)} fusion(bf16[1024,8192]{1,0:T(8,128)(2,1)} %constant_dynamic-update-slice_fusion, bf16[8,8192]{1,0:T(8,128)(2,1)S(1)} %bitcast.35), kind=kOutput, calls=%fused_computation.5 | convolution fusion | flops 134225920 | bytes 16924672 | tf_op jit(solution)/shard_map/dot_general | solution.py:31
  255.8 33.7 %all-reduce = bf16[8,1024]{1,0:T(8,128)(2,1)S(1)} all-reduce(bf16[8,1024]{1,0:T(8,128)(2,1)S(1)} %fusion.3), channel_id=2, replica_groups=mesh['layer'=8,'land'=4] {'layer'}, use_global_device_ids=true, to_apply=%region_0.1.clone | all-reduce | flops 8192 | bytes 32768
  289.5 0.6 dynamic-slice_bitcast_fusion.1
  290.1 5.2 %all-gather = bf16[4,1,1024]{2,1,0:T(2,128)(2,1)S(1)} all-gather(bf16[1,1,1024]{2,1,0:T(2,128)(2,1)S(1)} %dynamic-slice_bitcast_fusion.1), channel_id=1, replica_groups=mesh['layer'=8,'land'=4] {'land'}, dimensions={0}, use_global_device_ids=true | all-gather | bytes 10240 | tf_op jit(solution)/shard_map/all_gather | solution.py:67
  295.3 0.0 copy-done
  295.3 0.2 fusion.6
  295.5 26.0 %all-gather.1 = bf16[8,4,256]{2,1,0:T(4,128)(2,1)S(1)} all-gather(bf16[1,4,256]{2,1,0:T(4,128)(2,1)S(1)} %fusion.6), channel_id=1, replica_groups=mesh['layer'=8,'land'=4] {'layer'}, dimensions={0}, use_global_device_ids=true | all-gather | bytes 18432 | tf_op jit(solution)/shard_map/all_gather | solution.py:75
  321.5 0.0 collective-permute-done.3
  321.5 0.2 concatenate
  321.8 6.2 %all-gather.2 = bf16[4,30,1024]{2,1,0:T(8,128)(2,1)S(1)} all-gather(bf16[1,30,1024]{2,1,0:T(8,128)(2,1)S(1)} %dynamic-slice_bitcast_fusion), channel_id=1, replica_groups=mesh['layer'=8,'land'=4] {'land'}, dimensions={0}, use_global_device_ids=true | all-gather | bytes 307200 | tf_op jit(solution)/shard_map/all_gather | solution.py:66
  328.0 0.1 reshape.26
  328.1 0.3 fusion.5
  328.4 7.2 %all-reduce.2 = bf16[32,120]{1,0:T(8,128)(2,1)S(1)} all-reduce(bf16[32,120]{1,0:T(8,128)(2,1)S(1)} %fusion.5), channel_id=4, replica_groups=mesh['layer'=8,'land'=4] {'land'}, use_global_device_ids=true, to_apply=%region_2.3.clone | all-reduce | flops 3840 | bytes 15360
  335.6 0.6 dynamic-slice_convert_fusion
  (3 shorter events, 0.1 us)
Async XLA Ops:
  0.0 295.3 %copy-start = (bf16[1024,256]{1,0:T(8,128)(2,1)S(1)}, bf16[1024,256]{1,0:T(8,128)(2,1)}, u32[]{:S(2)}) copy-start(bf16[1024,256]{1,0:T(8,128)(2,1)} %param.7) | copy-start | bytes 1572868
  0.0 110.8 %copy-start.4 = (u32[32]{0:T(128)S(1)}, u32[32]{0:T(128)}, u32[]{:S(2)}) copy-start(u32[32]{0:T(128)} %constant.51) | copy-start | bytes 388
  0.0 111.3 %copy-start.3 = (u32[32]{0:T(128)S(1)}, u32[32]{0:T(128)}, u32[]{:S(2)}) copy-start(u32[32]{0:T(128)} %constant.43) | copy-start | bytes 388
  0.0 109.9 %copy-start.2 = (bf16[32,2048]{1,0:T(8,128)(2,1)S(1)}, bf16[32,2048]{1,0:T(8,128)(2,1)}, u32[]{:S(2)}) copy-start(bf16[32,2048]{1,0:T(8,128)(2,1)} %param.5) | copy-start | bytes 393220
  0.0 91.3 %collective-permute-start = (bf16[1024,2048]{1,0:T(8,128)(2,1)}, bf16[1024,2048]{1,0:T(8,128)(2,1)}, u32[]{:S(2)}, u32[]{:S(2)}) collective-permute-start(bf16[1024,2048]{1,0:T(8,128)(2,1)} %param.6), channel_id=1, source_target_pairs={{0,1},{1,2},{2,3},{3,0},{4,5},{5,6},{6,7},{7,4},{8,9},{9,10},{10,1... | collective-permute-start | bytes 12582920 | tf_op jit(solution)/shard_map/ppermute | solution.py:18
  0.5 200.7 %collective-permute-start.1 = (bf16[1024,2048]{1,0:T(8,128)(2,1)}, bf16[1024,2048]{1,0:T(8,128)(2,1)}, u32[]{:S(2)}, u32[]{:S(2)}) collective-permute-start(bf16[1024,2048]{1,0:T(8,128)(2,1)} %param.6), channel_id=1, source_target_pairs={{0,3},{1,0},{2,1},{3,2},{4,7},{5,4},{6,5},{7,6},{8,11},{9,8},{10,9... | collective-permute-start | bytes 12582920 | tf_op jit(solution)/shard_map/ppermute | solution.py:23
  91.3 114.6 %collective-permute-start.2 = (bf16[1024,2048]{1,0:T(8,128)(2,1)}, bf16[1024,2048]{1,0:T(8,128)(2,1)}, u32[]{:S(2)}, u32[]{:S(2)}) collective-permute-start(bf16[1024,2048]{1,0:T(8,128)(2,1)} %collective-permute-done), channel_id=1, source_target_pairs={{0,1},{1,2},{2,3},{3,0},{4,5},{5,6},{6,7},{7,4},{8,9},{9,10},{10,1... | collective-permute-start | bytes 12582920 | tf_op jit(solution)/shard_map/ppermute | solution.py:18
  105.0 66.1 %all-to-all-start.1 = ((bf16[8,4,30,2048]{3,0,2,1:T(8,128)(2,1)}), bf16[8,4,30,2048]{3,0,2,1:T(8,128)(2,1)}, u32[]{:S(2)}, u32[]{:S(2)}) async-start(bf16[8,4,30,2048]{3,0,2,1:T(8,128)(2,1)} %copy.9), calls=%async_computation.1 | async-start | bytes 7864320 | tf_op jit(solution)/shard_map/all_to_all | solution.py:49
  113.2 6.7 %copy-start.1 = (bf16[1024,2048]{1,0:T(8,128)(2,1)S(1)}, bf16[1024,2048]{1,0:T(8,128)(2,1)}, u32[]{:S(2)}) copy-start(bf16[1024,2048]{1,0:T(8,128)(2,1)} %param.6) | copy-start | bytes 12582916
  171.1 74.5 %all-to-all-start = ((bf16[8,4,1,2048]{3,0,2,1:T(8,128)(2,1)}), bf16[8,4,1,2048]{3,0,2,1:T(8,128)(2,1)S(1)}, u32[]{:S(2)}, u32[]{:S(2)}) async-start(bf16[8,4,1,2048]{3,0,2,1:T(8,128)(2,1)} %copy.8), calls=%async_computation | async-start | bytes 262144 | tf_op jit(solution)/shard_map/all_to_all | solution.py:50
  243.9 77.7 %collective-permute-start.3 = (bf16[14,1024]{1,0:T(8,128)(2,1)S(1)}, bf16[14,1024]{1,0:T(8,128)(2,1)S(1)}, u32[]{:S(2)}, u32[]{:S(2)}) collective-permute-start(bf16[14,1024]{1,0:T(8,128)(2,1)S(1)} %slice), channel_id=1, source_target_pairs={{0,4},{4,8},{8,12},{12,16},{16,20},{20,24},{24,28},{1,5},{5,9},{9,... | collective-permute-start | bytes 86024
